TPU v7x, 256 devices: a whole 4x4x8 slice. The times are simulated.
256 devices in a mesh: tm: 8 (over y, x_hi), space: 32 (over z, x_lo, core).
Axes of the slice: x: 4 (x_hi: 2, x_lo: 2; x = x_hi * 2 + x_lo), y: 4, z: 8, core: 2. Of those that a mesh axis runs over, the one named last changes fastest.
Arguments:
- wave_field: bfloat16 [16, 8192, 256], P('tm', 'space'), may hold values from -600 to 600
- cotangent: bfloat16 [16, 8192, 256], P('tm', 'space'), may hold values from -6 to 6
- block_lists: int32 [16, 64, 4], P('tm', 'space'), may hold values from 0 to 63, as said below
- project_weights: bfloat16 [2, 256, 768], replicated, may hold values from -2 to 2
- combine_weights: bfloat16 [2, 256, 256], replicated, may hold values from -0.375 to 0.375
Outputs:
- mixed_field: bfloat16 [16, 8192, 256], P('tm', 'space')
- field_grad: bfloat16 [16, 8192, 256], P('tm', 'space')
- project_grad: float32 [2, 256, 768], replicated
- combine_grad: float32 [2, 256, 256], replicated
Inputs may be any that keep to these rules, and one draw needn't show every extreme that they name: `block_lists`: for frame f and block b, entry 0 is b itself, entry 1 is b - 2 or b + 2, and every entry lies within 2 blocks of b; entries may repeat.
All inputs are finite; a program needn't handle non-finite values.
Results may differ from a plain program's by a relative error of at most 0.012.
Values may be sent and summed in bfloat16 or wider, within the bound.
A program may use at most 128 MiB of HBM per device.

v0:
```python
import math
import jax
import jax.numpy as jnp
from jax import lax
from jax.sharding import PartitionSpec as P

HEADS = 8
BLOCK = 128
HREACH = 2
epsilon = 1e-05


def with_halo(cells, sides, width):
    for axis, dim in sides:
        count = lax.axis_size(axis)
        ends = count - 1
        head = lax.slice_in_dim(cells, 0, width, axis=dim)
        tail = lax.slice_in_dim(cells, cells.shape[dim] - width, cells.shape[dim], axis=dim)
        cells = jnp.concatenate(
            [
                lax.ppermute(tail, axis, [(i, (i + 1) % count) for i in range(ends)]),
                cells,
                lax.ppermute(head, axis, [((i + 1) % count, i) for i in range(ends)]),
            ],
            axis=dim,
        )
    return cells


def layer_norm(tok_rows):
    widened = tok_rows.astype(jnp.float32)
    centered = widened - jnp.mean(widened, axis=-1, keepdims=True)
    inverse = lax.rsqrt(jnp.mean(centered * centered, axis=-1, keepdims=True) + epsilon)
    return (centered * inverse, inverse)


def norm_backward(upstream, normed, inverse):
    mean_grad = jnp.mean(upstream, axis=-1, keepdims=True)
    mean_cross = jnp.mean(upstream * normed, axis=-1, keepdims=True)
    return inverse * (upstream - mean_grad - normed * mean_cross)


def matmul(left_op, right_op):
    return jnp.dot(left_op, right_op, preferred_element_type=jnp.float32)


def wide_dot(left_op, right_op):
    return jnp.dot(
        left_op.astype(jnp.float32), right_op.astype(jnp.float32), precision=lax.Precision.HIGHEST
    )


def matmul_left(left_op, right_op):
    return lax.dot_general(
        left_op, right_op, (((0,), (0,)), ((), ())), preferred_element_type=jnp.float32
    )


def matmul_right(left_op, right_op):
    return lax.dot_general(
        left_op, right_op, (((1,), (1,)), ((), ())), preferred_element_type=jnp.float32
    )


def einsum_wide(formula, left_op, right_op):
    return jnp.einsum(formula, left_op, right_op, preferred_element_type=jnp.float32)


def softmax_rows(scores, reduce_axis):
    row_max = jnp.max(scores, axis=reduce_axis, keepdims=True)
    exp_scores = jnp.exp(scores - row_max)
    return lax.optimization_barrier(
        (exp_scores / jnp.sum(exp_scores, axis=reduce_axis, keepdims=True)).astype(jnp.bfloat16)
    )


def temporal_pair(tok_rows, cot_rows, project, combine, score_scale):
    frame_count, row_count, features = tok_rows.shape
    head_width = features // HEADS
    normed, inverse = layer_norm(tok_rows)
    normed_act = normed.astype(jnp.bfloat16).reshape(frame_count * row_count, features)
    projected = (
        matmul(normed_act, project)
        .astype(jnp.bfloat16)
        .reshape(frame_count, row_count, 3, HEADS, head_width)
    )
    queries = projected[:, :, 0]
    key_part = projected[:, :, 1]
    value_part = projected[:, :, 2]
    attn_probs = softmax_rows(einsum_wide("frhe,grhe->hfgr", queries, key_part) * score_scale, 2)
    attended = (
        einsum_wide("hfgr,grhe->frhe", attn_probs, value_part)
        .astype(jnp.bfloat16)
        .reshape(frame_count * row_count, features)
    )
    mixed = (
        tok_rows.astype(jnp.float32)
        + matmul(attended, combine).reshape(frame_count, row_count, features)
    ).astype(jnp.bfloat16)
    flat_cot = cot_rows.reshape(frame_count * row_count, features)
    outward = matmul_left(attended, flat_cot)
    attn_grad = (
        matmul_right(flat_cot, combine)
        .astype(jnp.bfloat16)
        .reshape(frame_count, row_count, HEADS, head_width)
    )
    grad_probs = einsum_wide("frhe,grhe->hfgr", attn_grad, value_part)
    prob_wide = attn_probs.astype(jnp.float32)
    row_delta = jnp.sum(prob_wide * grad_probs, axis=2, keepdims=True)
    grad_scores = (prob_wide * (grad_probs - row_delta) * score_scale).astype(jnp.bfloat16)
    grad_query = einsum_wide("hfgr,grhe->frhe", grad_scores, key_part)
    grad_keys = einsum_wide("hfgr,frhe->grhe", grad_scores, queries)
    grad_values = einsum_wide("hfgr,frhe->grhe", attn_probs, attn_grad)
    project_rows = (
        jnp.stack([grad_query, grad_keys, grad_values], axis=2)
        .astype(jnp.bfloat16)
        .reshape(frame_count * row_count, 3 * features)
    )
    inward = matmul_left(normed_act, project_rows)
    act_grad = matmul_right(project_rows, project).reshape(frame_count, row_count, features)
    field_rows = (cot_rows.astype(jnp.float32) + norm_backward(act_grad, normed, inverse)).astype(
        jnp.bfloat16
    )
    return (mixed, field_rows, inward, outward)


def owner_sums(tile_sums, edge_sums, rim_rows, row_count):
    arrived = with_halo(edge_sums.astype(jnp.bfloat16), (("space", 1),), rim_rows).astype(
        edge_sums.dtype
    )
    pair_grad = tile_sums[:, rim_rows : rim_rows + row_count]
    pair_grad = pair_grad + arrived[:, :rim_rows]
    pair_grad = pair_grad + arrived[:, 3 * rim_rows :]
    return pair_grad


def per_device(wave_field, cotangent, block_lists, project_weights, combine_weights):
    frame_count, row_count, features = wave_field.shape
    head_width = features // HEADS
    score_scale = 1.0 / math.sqrt(head_width)
    block_count = row_count // BLOCK
    list_length = block_lists.shape[-1]
    rim_rows = HREACH * BLOCK
    padded_blocks = block_count + 2 * HREACH
    group_count = frame_count * block_count // 4
    space_project = project_weights[0]
    space_combine = combine_weights[0]
    normed, inverse = layer_norm(wave_field)
    normed_act = normed.astype(jnp.bfloat16)
    flat_act = normed_act.reshape(frame_count * row_count, features)
    projected = (
        matmul(flat_act, space_project)
        .astype(jnp.bfloat16)
        .reshape(frame_count, row_count, 3 * features)
    )
    keys_values = projected[:, :, features:]
    extended = with_halo(keys_values, (("space", 1),), rim_rows)
    first_block = lax.axis_index("space") * block_count - HREACH
    frame_base = (jnp.arange(frame_count, dtype=jnp.int32) * padded_blocks)[:, None, None]
    group_index = (block_lists - first_block + frame_base).reshape(group_count, 4 * list_length)
    padded_flat = extended.reshape(frame_count * padded_blocks, BLOCK, 2, HEADS, head_width)
    queries = projected[:, :, :features].reshape(group_count, 4, BLOCK, HEADS, head_width)

    def group_weights(group_query, group_rows):
        picked = jnp.take(padded_flat, group_rows, axis=0).reshape(
            4, list_length * BLOCK, 2, HEADS, head_width
        )
        scores = einsum_wide("gqhe,gkhe->ghqk", group_query, picked[:, :, 0]) * score_scale
        return (picked, softmax_rows(scores, 3))

    def forward_group(element):
        picked, attn_probs = group_weights(element[0], element[1])
        return einsum_wide("ghqk,gkhe->gqhe", attn_probs, picked[:, :, 1]).astype(jnp.bfloat16)

    attended = lax.map(forward_group, (queries, group_index)).reshape(
        frame_count * row_count, features
    )
    mixed_space = (
        wave_field.astype(jnp.float32)
        + matmul(attended, space_combine).reshape(frame_count, row_count, features)
    ).astype(jnp.bfloat16)
    history, history_cot = (
        lax.all_to_all(mixed_space, "tm", split_axis=1, concat_axis=0, tiled=True),
        lax.all_to_all(cotangent, "tm", split_axis=1, concat_axis=0, tiled=True),
    )
    time_mixed, time_grad, time_inward, time_outward = temporal_pair(
        history, history_cot, project_weights[1], combine_weights[1], score_scale
    )
    mixed_field, mixed_grad = (
        lax.all_to_all(time_mixed, "tm", split_axis=0, concat_axis=1, tiled=True),
        lax.all_to_all(time_grad, "tm", split_axis=0, concat_axis=1, tiled=True),
    )
    flat_grad = mixed_grad.reshape(frame_count * row_count, features)
    space_outward = matmul_left(attended, flat_grad)
    attn_grad = (
        matmul_right(flat_grad, space_combine)
        .astype(jnp.bfloat16)
        .reshape(group_count, 4, BLOCK, HEADS, head_width)
    )

    def backward_group(running, element):
        group_query, group_rows, group_grad = element
        picked, attn_probs = group_weights(group_query, group_rows)
        key_part = picked[:, :, 0]
        value_part = picked[:, :, 1]
        prob_wide = attn_probs.astype(jnp.float32)
        grad_probs = einsum_wide("gqhe,gkhe->ghqk", group_grad, value_part)
        row_delta = jnp.sum(prob_wide * grad_probs, axis=3, keepdims=True)
        grad_scores = (prob_wide * (grad_probs - row_delta) * score_scale).astype(jnp.bfloat16)
        grad_query = einsum_wide("ghqk,gkhe->gqhe", grad_scores, key_part).astype(jnp.bfloat16)
        grad_keys = einsum_wide("ghqk,gqhe->gkhe", grad_scores, group_query)
        grad_values = einsum_wide("ghqk,gqhe->gkhe", attn_probs, group_grad)
        key_tiles = jnp.stack([grad_keys, grad_values], axis=2).reshape(
            4 * list_length, BLOCK * 2 * features
        )
        return (running.at[group_rows].add(key_tiles), grad_query)

    zero_tiles = jnp.zeros((frame_count * padded_blocks, BLOCK * 2 * features), jnp.float32)
    tile_sums, grad_query = lax.scan(backward_group, zero_tiles, (queries, group_index, attn_grad))
    tile_sums = tile_sums.reshape(frame_count, row_count + 2 * rim_rows, 2 * features)
    edge_sums = jnp.concatenate(
        [tile_sums[:, :rim_rows], tile_sums[:, rim_rows + row_count :]], axis=1
    )
    kv_project = space_project[:, features:]
    query_flat = grad_query.reshape(frame_count * row_count, features)
    pair_grad = owner_sums(tile_sums, edge_sums, rim_rows, row_count)
    pair_flat = pair_grad.reshape(frame_count * row_count, 2 * features)
    space_inward = jnp.concatenate(
        [matmul_left(flat_act, query_flat), wide_dot(flat_act.T, pair_flat)], axis=1
    )
    act_grad = matmul_right(query_flat, space_project[:, :features]) + wide_dot(
        pair_flat, kv_project.T
    )
    act_grad = act_grad.reshape(frame_count, row_count, features)
    field_grad = (mixed_grad.astype(jnp.float32) + norm_backward(act_grad, normed, inverse)).astype(
        jnp.bfloat16
    )
    space_inward, space_outward, time_inward, time_outward = lax.psum(
        (space_inward, space_outward, time_inward, time_outward), ("tm", "space")
    )
    factor = 1.0 / math.sqrt(frame_count * row_count * lax.axis_size("tm") * lax.axis_size("space"))
    project_grad = jnp.stack([space_inward, time_inward]) * factor
    combine_grad = jnp.stack([space_outward, time_outward]) * factor
    return (mixed_field, field_grad, project_grad, combine_grad)


def solution(mesh):
    in_specs = (P("tm", "space", None), P("tm", "space", None), P("tm", "space", None), P(), P())
    out_specs = (P("tm", "space", None), P("tm", "space", None), P(), P())
    return jax.shard_map(
        per_device, mesh=mesh, in_specs=in_specs, out_specs=out_specs, check_vma=False
    )
```

profile of v0, /device:TPU:2, one launch (start us, length us, event | category | flops | bytes accessed | tf_op | source)
XLA Modules:
  0.0 562.2 jit_solution(7572471238798868176)
XLA Ops:
  13.4 1.9 collective-permute-start.1
  15.3 2.4 collective-permute-start
  18.7 6.0 %all-to-all-start.2 = ((bf16[2,256,256]{2,0,1:T(2,128)(2,1)}), bf16[2,256,256]{2,0,1:T(2,128)(2,1)S(1)}, u32[]{:S(2)}, u32[]{:S(2)}) async-start(bf16[2,256,256]{2,0,1:T(2,128)(2,1)} %copy.163), calls=%async_computation.2 | async-start | bytes 524288 | tf_op jit(solution)/shard_map/all_to_all | solution.py:184
  26.2 8.0 %all-to-all-done.2 = bf16[2,256,256]{2,0,1:T(2,128)(2,1)S(1)} async-done(((bf16[2,256,256]{2,0,1:T(2,128)(2,1)}), bf16[2,256,256]{2,0,1:T(2,128)(2,1)S(1)}, u32[]{:S(2)}, u32[]{:S(2)}) %all-to-all-start.2) | async-done | bytes 262176 | tf_op jit(solution)/shard_map/all_to_all | solution.py:184
  34.3 3.1 pad_maximum_fusion.2
  37.3 2.1 reshape.238
  39.4 2.0 copy.145
  41.4 2.2 gather_fusion
  43.6 1.9 broadcast_select_fusion
  45.4 2.7 copy.146
  48.1 2.7 reshape.239
  54.0 6.7 %fusion.100 = (f32[4,8,128]{2,1,0:T(8,128)S(1)}, f32[4,8,128,512]{3,2,1,0:T(8,128)S(1)}) fusion(f32[4,8,128,512]{3,2,1,0:T(8,128)S(1)} %fusion.42), kind=kOutput, calls=%fused_computation.168 | output fusion | flops 8389119 | bytes 16793600 | tf_op jit(solution)/shard_map/while/body/eval_jaxpr/sub | solution.py:71
  61.5 2.0 copy-done
  63.4 1.5 fusion.30
  66.6 3.7 all-to-all-start
  72.0 8.0 %all-to-all-done = bf16[2,256,256]{2,0,1:T(2,128)(2,1)S(1)} async-done(((bf16[2,256,256]{2,0,1:T(2,128)(2,1)}), bf16[2,256,256]{2,0,1:T(2,128)(2,1)S(1)}, u32[]{:S(2)}, u32[]{:S(2)}) %all-to-all-start) | async-done | bytes 262176 | tf_op jit(solution)/shard_map/all_to_all | solution.py:183
  83.5 3.6 reshape.240
  87.1 2.7 slice_bitcast_fusion.3
  89.8 3.7 fusion.37
  93.5 3.3 divide_convert_fusion.1
  99.4 1.4 dot_general.98
  102.1 2.4 fusion.34
  106.5 11.7 %fusion.24 = bf16[16,32,1,8,32]{4,0,3,1,2:T(8,128)(2,1)S(1)} fusion(bf16[16,32,8,32]{3,2,1,0:T(8,128)(2,1)S(1)} %copy-done.8, bf16[8,16,16,32]{1,2,3,0:T(8,128)(2,1)S(1)} %fusion.15), kind=kOutput, calls=%fused_computation.45 | convolution fusion | flops 4325376 | bytes 655360 | tf_op jit(solution)/shard_map/hfgr,grhe->frhe/dot_general | solution.py:66
  119.8 2.8 convert_element_type.178
  122.6 2.8 convert_element_type.167
  126.6 2.0 convolution_bitcast_fusion.3
  128.7 2.5 convolution_bitcast_fusion.1
  133.0 3.4 all-to-all-start.3
  136.4 1.8 fusion.29
  138.3 6.9 %all-to-all-done.3 = bf16[16,32,256]{2,1,0:T(8,128)(2,1)S(1)} async-done(((bf16[16,32,256]{2,1,0:T(8,128)(2,1)}), bf16[16,32,256]{2,1,0:T(8,128)(2,1)S(1)}, u32[]{:S(2)}, u32[]{:S(2)}) %all-to-all-start.3) | async-done | bytes 262176 | tf_op jit(solution)/shard_map/all_to_all | solution.py:191
  145.1 4.0 all-to-all-start.1
  150.5 2.9 convolution_bitcast_fusion
  153.4 4.5 fusion.41
  158.0 11.7 %fusion.21 = f32[4,512,1,8,32]{1,4,3,0,2:T(8,128)} fusion(bf16[4,8,128,512]{3,2,1,0:T(8,128)(2,1)} %copy-done, f32[4,8,128,512]{3,2,1,0:T(8,128)} %fusion.41, bf16[4,128,8,32]{1,0,3,2:T(4,128)(2,1)S(1)} %copy-done.26), kind=kOutput, calls=%fused_computation.33 | convolution fusion | flops 148902400 | bytes 14942208 | tf_op jit(solution)/shard_map/while/body/eval_jaxpr/ghqk,gqhe->gkhe/dot_general | solution.py:66
  169.7 4.1 pad_maximum_fusion
  173.8 12.6 %copy.182 = f32[4,512,2,8,32]{4,3,2,1,0:T(8,128)} copy(f32[4,512,2,8,32]{1,4,3,0,2:T(8,128)} %pad_maximum_fusion) | data formatting | bytes 8388608 | tf_op jit(solution)/shard_map/while/body/eval_jaxpr/stack | solution.py:213
  186.4 16.9 %reshape.268 = f32[16,65536]{1,0:T(8,128)} reshape(f32[4,512,2,8,32]{4,3,2,1,0:T(8,128)} %copy.182) | data formatting | bytes 8388608 | tf_op jit(solution)/shard_map/while/body/eval_jaxpr/reshape | solution.py:213
  203.3 2.2 broadcast_in_dim.24
  205.5 38.1 %scatter_fusion = f32[12,65536]{1,0:T(8,128)} fusion(f32[12,65536]{1,0:T(8,128)} %broadcast_in_dim.24, s32[16]{0:T(128)S(1)} %fusion.91, f32[16,65536]{1,0:T(8,128)} %reshape.268), kind=kCustom, calls=%fused_computation.1 | custom fusion | flops 1048576 | bytes 12582976 | tf_op jit(solution)/shard_map/while/body/eval_jaxpr/scatter-add | solution.py:216
  243.6 2.8 reshape.246
  247.6 11.5 %fusion.31 = bf16[4,128,8,32]{1,3,2,0:T(8,128)(2,1)} fusion(bf16[4,8,128,512]{3,2,1,0:T(8,128)(2,1)} %copy-done, f32[4,8,128,512]{3,2,1,0:T(8,128)} %fusion.41, bf16[4,512,1,8,32]{1,0,4,3,2:T(4,128)(2,1)} %copy-done.6), kind=kOutput, calls=%fused_computation.62 | convolution fusion | flops 149033472 | bytes 13893632 | tf_op jit(solution)/shard_map/while/body/eval_jaxpr/ghqk,gkhe->gqhe/dot_general | solution.py:66
  259.1 2.2 collective-permute-start.2
  261.3 4.6 collective-permute-start.3
  265.9 2.0 convolution_bitcast_fusion.4
  267.8 1.7 copy.162
  271.9 2.0 fusion.70
  280.7 270.7 %all-reduce.3.cloned.1.call-done = (f32[1,256,768]{2,1,0:T(8,128)}, f32[1,256,768]{2,1,0:T(8,128)}, f32[1,256,256]{2,1,0:T(8,128)}, f32[1,256,256]{2,1,0:T(8,128)}) async-done(((f32[1,256,768]{2,1,0:T(8,128)}, f32[1,256,768]{2,1,0:T(8,128)}, f32[1,256,256]{2,1,0:T(8,128)}, f32[1,256,256]{2,1,0:T(8,128)}), (f32[1,256,768]{2,1,0:T(8,128)}, f32[1,256,768]{2,1,0:T(8,128)}, f32[1,256,256]{2,1,0:T(8,128)}, ...) | async-done | bytes 2097168 | tf_op jit(solution)/shard_map/psum | solution.py:238
  551.4 2.7 maximum_multiply_fusion
  (148 shorter events, 41.9 us)
Async XLA Ops:
  7.2 17.6 %copy-start.18 = (bf16[2,256,768]{2,1,0:T(8,128)(2,1)S(1)}, bf16[2,256,768]{2,1,0:T(8,128)(2,1)}, u32[]{:S(2)}) copy-start(bf16[2,256,768]{2,1,0:T(8,128)(2,1)} %param.10) | copy-start | bytes 2359300
  7.2 10.5 %copy-start.31 = (bf16[2,256,256]{2,1,0:T(8,128)(2,1)S(1)}, bf16[2,256,256]{2,1,0:T(8,128)(2,1)}, u32[]{:S(2)}) copy-start(bf16[2,256,256]{2,1,0:T(8,128)(2,1)} %param.8) | copy-start | bytes 786436
  8.4 17.1 %copy-start.34 = (s32[2,2,4]{2,1,0:T(2,128)S(1)}, s32[2,2,4]{2,1,0:T(2,128)}, u32[]{:S(2)}) copy-start(s32[2,2,4]{2,1,0:T(2,128)} %param.9) | copy-start | bytes 196
  10.8 0.7 copy-start.15
  13.4 20.9 %collective-permute-start.1 = (bf16[2,256,512]{1,0,2:T(2,128)(2,1)S(1)}, bf16[2,256,512]{1,0,2:T(2,128)(2,1)}, u32[]{:S(2)}, u32[]{:S(2)}) collective-permute-start(bf16[2,256,512]{1,0,2:T(2,128)(2,1)S(1)} %copy.194), channel_id=1, source_target_pairs={{1,0},{2,1},{3,2},{4,3},{5,4},{6,5},{7,6},{8,7},{9,8},{10,9},{11,1... | collective-permute-start | bytes 1572872 | tf_op jit(solution)/shard_map/ppermute | solution.py:23
  15.3 19.0 %collective-permute-start = (bf16[2,256,512]{1,0,2:T(2,128)(2,1)S(1)}, bf16[2,256,512]{1,0,2:T(2,128)(2,1)}, u32[]{:S(2)}, u32[]{:S(2)}) collective-permute-start(bf16[2,256,512]{1,0,2:T(2,128)(2,1)S(1)} %copy.194), channel_id=1, source_target_pairs={{0,1},{1,2},{2,3},{3,4},{4,5},{5,6},{6,7},{7,8},{8,9},{9,10},{10,1... | collective-permute-start | bytes 1572872 | tf_op jit(solution)/shard_map/ppermute | solution.py:21
  18.7 15.5 %all-to-all-start.2 = ((bf16[2,256,256]{2,0,1:T(2,128)(2,1)}), bf16[2,256,256]{2,0,1:T(2,128)(2,1)S(1)}, u32[]{:S(2)}, u32[]{:S(2)}) async-start(bf16[2,256,256]{2,0,1:T(2,128)(2,1)} %copy.163), calls=%async_computation.2 | async-start | bytes 524288 | tf_op jit(solution)/shard_map/all_to_all | solution.py:184
  26.2 25.5 %copy-start.25 = (bf16[4,128,8,32]{1,0,3,2:T(4,128)(2,1)}, bf16[4,128,8,32]{1,0,3,2:T(4,128)(2,1)S(1)}, u32[]{:S(2)}) copy-start(bf16[4,128,8,32]{1,0,3,2:T(4,128)(2,1)S(1)} %squeeze.57) | copy-start | bytes 786436
  34.2 36.1 %copy-start.11 = (bf16[2,8,32,256]{3,2,0,1:T(8,128)(2,1)}, bf16[2,8,32,256]{3,2,0,1:T(8,128)(2,1)S(1)}, u32[]{:S(2)}) copy-start(bf16[2,8,32,256]{3,2,0,1:T(8,128)(2,1)S(1)} %copy.164) | copy-start | bytes 786436
  51.7 1.0 copy-start.6
  51.7 9.8 %copy-start.1 = (bf16[4,512,1,8,32]{1,0,4,3,2:T(4,128)(2,1)}, bf16[4,512,1,8,32]{1,0,4,3,2:T(4,128)(2,1)S(1)}, u32[]{:S(2)}) copy-start(bf16[4,512,1,8,32]{1,0,4,3,2:T(4,128)(2,1)S(1)} %get-tuple-element.53) | copy-start | bytes 3145732
  61.4 2.0 copy-start
  63.4 1.9 copy-start.7
  63.4 1.9 copy-start.29
  65.2 16.3 %copy-start.22 = (bf16[4,128,8,32]{1,0,3,2:T(4,128)(2,1)}, bf16[4,128,8,32]{1,0,3,2:T(4,128)(2,1)S(1)}, u32[]{:S(2)}) copy-start(bf16[4,128,8,32]{1,0,3,2:T(4,128)(2,1)S(1)} %copy.151) | copy-start | bytes 786436
  65.4 16.9 %copy-start.19 = (bf16[2,256,768]{2,1,0:T(8,128)(2,1)S(1)}, bf16[2,256,768]{2,1,0:T(8,128)(2,1)}, u32[]{:S(2)}) copy-start(bf16[2,256,768]{2,1,0:T(8,128)(2,1)} %param.10) | copy-start | bytes 2359300
  66.6 13.4 %all-to-all-start = ((bf16[2,256,256]{2,0,1:T(2,128)(2,1)}), bf16[2,256,256]{2,0,1:T(2,128)(2,1)S(1)}, u32[]{:S(2)}, u32[]{:S(2)}) async-start(bf16[2,256,256]{2,0,1:T(2,128)(2,1)} %copy.153), calls=%async_computation | async-start | bytes 524288 | tf_op jit(solution)/shard_map/all_to_all | solution.py:183
  81.5 0.7 copy-start.23
  93.5 3.3 copy-start.10
  97.7 3.1 copy-start.3
  100.8 1.2 copy-start.17
  104.4 1.2 copy-start.9
  104.4 2.1 copy-start.8
  125.4 6.0 %copy-start.20 = (bf16[2,256,768]{2,1,0:T(8,128)(2,1)S(1)}, bf16[2,256,768]{2,1,0:T(8,128)(2,1)}, u32[]{:S(2)}) copy-start(bf16[2,256,768]{2,1,0:T(8,128)(2,1)} %param.10) | copy-start | bytes 2359300
  125.4 6.0 %copy-start.21 = (bf16[16,32,768]{2,1,0:T(8,128)(2,1)S(1)}, bf16[16,32,768]{2,1,0:T(8,128)(2,1)}, u32[]{:S(2)}) copy-start(bf16[16,32,768]{2,1,0:T(8,128)(2,1)} %convert_element_type.167) | copy-start | bytes 2359300
  126.6 5.3 copy-start.12
  131.2 5.2 copy-start.28
  131.9 18.1 %copy-start.30 = (bf16[2,256,256]{2,1,0:T(8,128)(2,1)S(1)}, bf16[2,256,256]{2,1,0:T(8,128)(2,1)}, u32[]{:S(2)}) copy-start(bf16[2,256,256]{2,1,0:T(8,128)(2,1)} %param.11) | copy-start | bytes 786436
  133.0 12.1 %all-to-all-start.3 = ((bf16[16,32,256]{2,1,0:T(8,128)(2,1)}), bf16[16,32,256]{2,1,0:T(8,128)(2,1)S(1)}, u32[]{:S(2)}, u32[]{:S(2)}) async-start(bf16[16,32,256]{2,1,0:T(8,128)(2,1)} %fusion.58), calls=%async_computation.3 | async-start | bytes 524288 | tf_op jit(solution)/shard_map/all_to_all | solution.py:191
  145.1 122.7 %all-to-all-start.1 = ((bf16[16,32,256]{2,1,0:T(8,128)(2,1)}), bf16[16,32,256]{2,1,0:T(8,128)(2,1)}, u32[]{:S(2)}, u32[]{:S(2)}) async-start(bf16[16,32,256]{2,1,0:T(8,128)(2,1)} %fusion.29), calls=%async_computation.1 | async-start | bytes 524288 | tf_op jit(solution)/shard_map/all_to_all | solution.py:190
  149.2 402.2 %all-reduce.3.cloned.1.call-start = ((), (), s32[]{:S(2)}) async-start(), calls=%async_computation.4 | async-start | bytes 4194304 | tf_op jit(solution)/shard_map/psum | solution.py:238
  149.3 0.7 copy-start.13
  150.4 3.0 copy-start.2
  153.4 4.5 copy-start.26
  259.1 14.8 %collective-permute-start.2 = (bf16[2,256,512]{2,1,0:T(8,128)(2,1)}, bf16[2,256,512]{2,1,0:T(8,128)(2,1)}, u32[]{:S(2)}, u32[]{:S(2)}) collective-permute-start(bf16[2,256,512]{2,1,0:T(8,128)(2,1)} %get-tuple-element.55), channel_id=1, source_target_pairs={{0,1},{1,2},{2,3},{3,4},{4,5},{5,6},{6,7},{7,8},{8,9},{9,10},{10,1... | collective-permute-start | bytes 1572872 | tf_op jit(solution)/shard_map/ppermute | solution.py:21
  261.3 12.6 %collective-permute-start.3 = (bf16[2,256,512]{2,1,0:T(8,128)(2,1)}, bf16[2,256,512]{2,1,0:T(8,128)(2,1)}, u32[]{:S(2)}, u32[]{:S(2)}) collective-permute-start(bf16[2,256,512]{2,1,0:T(8,128)(2,1)} %get-tuple-element.56), channel_id=1, source_target_pairs={{1,0},{2,1},{3,2},{4,3},{5,4},{6,5},{7,6},{8,7},{9,8},{10,9},{11,1... | collective-permute-start | bytes 1572872 | tf_op jit(solution)/shard_map/ppermute | solution.py:23
  269.5 6.8 %copy-start.16 = (bf16[2,256,256]{2,1,0:T(8,128)(2,1)S(1)}, bf16[2,256,256]{2,1,0:T(8,128)(2,1)}, u32[]{:S(2)}) copy-start(bf16[2,256,256]{2,1,0:T(8,128)(2,1)} %copy-done.15) | copy-start | bytes 786436
  275.3 1.0 copy-start.4
  276.3 1.7 copy-start.24
  276.3 1.7 copy-start.27
  277.0 1.6 copy-start.5
  277.0 2.6 copy-start.14
  551.4 2.7 copy-start.32
  551.4 2.7 copy-start.33
Sparse Core Ops, SparseCore 0:
  278.1 273.2 all-reduce.2
where the time goes:
time: 571 us; the launch traced here: 562 us
  waiting for transfers between devices  294 us (51%)
  local copies, waits for them, and re-layouts  81.3 us (14%)
  other arithmetic  73.3 us (13%)
  matrix products  70.6 us (12%)
  starting transfers between devices  28.3 us (5%)
  between operations  15.3 us (3%)
    psum x1, waiting for transfers between devices, per_device(): lax.psum((space_inward, space_outward, time_inward, time_outward), ('tm',...  271 us
    dot_general x12, matrix products, einsum_wide(): jnp.einsum(formula, left_op, right_op, preferred_element_type=jnp.float32)  53.7 us
    scatter-add x1, other arithmetic, backward_group(): return (running.at[group_rows].add(key_tiles), grad_query)  38.1 us
    reshape x1, local copies, waits for them, and re-layouts, backward_group(): jnp.stack([grad_keys, grad_values], axis=2)  16.9 us
    another operation x1, local copies, waits for them, and re-layouts, backward_group(): jnp.stack([grad_keys, grad_values], axis=2)  12.6 us
  transfers between devices with their start and end apart: 9, of which 4 were waited for; matrix products, arithmetic and copies ran while one was open for 22% of the time, Pallas kernels for 0%

commit v1 on v0

--- a/solution.py
+++ b/solution.py
@@ -236,7 +236,7 @@
         jnp.bfloat16
     )
     space_inward, space_outward, time_inward, time_outward = lax.psum(
-        (space_inward, space_outward, time_inward, time_outward), ("tm", "space")
+        lax.psum((space_inward, space_outward, time_inward, time_outward), "tm"), "space"
     )
     factor = 1.0 / math.sqrt(frame_count * row_count * lax.axis_size("tm") * lax.axis_size("space"))
     project_grad = jnp.stack([space_inward, time_inward]) * factor

time: 571 us -> 628 us (1.100)
  the two profiles are of different devices: /device:TPU:2 before, /device:TPU:1 now
where the time goes in v1:
time: 628 us; the launch traced here: 619 us
  waiting for transfers between devices  361 us (57%)
  local copies, waits for them, and re-layouts  79 us (13%)
  other arithmetic  72.7 us (12%)
  matrix products  61.5 us (10%)
  starting transfers between devices  29.2 us (5%)
  between operations  15.2 us (2%)
    psum x1, waiting for transfers between devices, per_device(): lax.psum(lax.psum((space_inward, space_outward, time_inward, time_outward...  218 us
    psum x1, waiting for transfers between devices, per_device(): lax.psum((space_inward, space_outward, time_inward, time_outward), 'tm')  112 us
    dot_general x12, matrix products, einsum_wide(): jnp.einsum(formula, left_op, right_op, preferred_element_type=jnp.float32)  44.6 us
    scatter-add x1, other arithmetic, backward_group(): return (running.at[group_rows].add(key_tiles), grad_query)  37.6 us
    reshape x1, local copies, waits for them, and re-layouts, backward_group(): jnp.stack([grad_keys, grad_values], axis=2)  16.9 us
    another operation x1, local copies, waits for them, and re-layouts, backward_group(): jnp.stack([grad_keys, grad_values], axis=2)  12.8 us
  transfers between devices with their start and end apart: 10, of which 6 were waited for; matrix products, arithmetic and copies ran while one was open for 5% of the time, Pallas kernels for 0%

profile of v1, /device:TPU:1, one launch (start us, length us, event | category | flops | bytes accessed | tf_op | source)
XLA Modules:
  0.0 618.8 jit_solution(9270458105636629993)
XLA Ops:
  13.3 5.1 collective-permute-start.1
  18.4 1.9 collective-permute-start
  21.3 6.0 all-to-all-start.2
  28.0 10.6 %all-to-all-done.2 = bf16[2,256,256]{2,0,1:T(2,128)(2,1)S(1)} async-done(((bf16[2,256,256]{2,0,1:T(2,128)(2,1)}), bf16[2,256,256]{2,0,1:T(2,128)(2,1)S(1)}, u32[]{:S(2)}, u32[]{:S(2)}) %all-to-all-start.2) | async-done | bytes 262176 | tf_op jit(solution)/shard_map/all_to_all | solution.py:184
  38.6 2.9 pad_maximum_fusion.2
  41.5 2.1 reshape.238
  43.6 2.0 copy.145
  45.6 2.2 gather_fusion
  47.8 1.9 broadcast_select_fusion
  49.6 2.7 copy.146
  52.3 2.7 reshape.239
  58.1 6.7 %fusion.101 = (f32[4,8,128]{2,1,0:T(8,128)S(1)}, f32[4,8,128,512]{3,2,1,0:T(8,128)S(1)}) fusion(f32[4,8,128,512]{3,2,1,0:T(8,128)S(1)} %fusion.42), kind=kOutput, calls=%fused_computation.166 | output fusion | flops 8389119 | bytes 16793600 | tf_op jit(solution)/shard_map/while/body/eval_jaxpr/sub | solution.py:71
  65.6 1.9 copy-done
  67.6 1.5 fusion.30
  70.8 3.6 all-to-all-start
  76.1 7.4 %all-to-all-done = bf16[2,256,256]{2,0,1:T(2,128)(2,1)S(1)} async-done(((bf16[2,256,256]{2,0,1:T(2,128)(2,1)}), bf16[2,256,256]{2,0,1:T(2,128)(2,1)S(1)}, u32[]{:S(2)}, u32[]{:S(2)}) %all-to-all-start) | async-done | bytes 262176 | tf_op jit(solution)/shard_map/all_to_all | solution.py:183
  87.0 3.6 reshape.240
  90.6 2.7 slice_bitcast_fusion.3
  93.3 3.7 fusion.37
  97.0 3.4 divide_convert_fusion.1
  100.5 2.4 fusion.34
  107.7 3.2 convert_element_type.178
  111.0 2.8 convert_element_type.167
  114.9 2.5 fusion.23
  119.2 2.5 fusion.105
  123.5 3.4 all-to-all-start.3
  127.0 1.9 fusion.106
  128.9 6.4 %all-to-all-done.3 = bf16[16,32,256]{2,1,0:T(8,128)(2,1)S(1)} async-done(((bf16[16,32,256]{2,1,0:T(8,128)(2,1)}), bf16[16,32,256]{2,1,0:T(8,128)(2,1)S(1)}, u32[]{:S(2)}, u32[]{:S(2)}) %all-to-all-start.3) | async-done | bytes 262176 | tf_op jit(solution)/shard_map/all_to_all | solution.py:191
  137.5 2.9 convolution_bitcast_fusion
  140.4 4.5 fusion.41
  145.0 11.7 %fusion.21 = f32[4,512,1,8,32]{1,4,3,0,2:T(8,128)} fusion(bf16[4,8,128,512]{3,2,1,0:T(8,128)(2,1)} %copy-done, f32[4,8,128,512]{3,2,1,0:T(8,128)} %fusion.41, bf16[4,128,8,32]{1,0,3,2:T(4,128)(2,1)S(1)} %copy-done.31), kind=kOutput, calls=%fused_computation.33 | convolution fusion | flops 148902400 | bytes 14942208 | tf_op jit(solution)/shard_map/while/body/eval_jaxpr/ghqk,gqhe->gkhe/dot_general | solution.py:66
  156.7 4.2 pad_maximum_fusion
  160.8 12.8 %copy.182 = f32[4,512,2,8,32]{4,3,2,1,0:T(8,128)} copy(f32[4,512,2,8,32]{1,4,3,0,2:T(8,128)} %pad_maximum_fusion) | data formatting | bytes 8388608 | tf_op jit(solution)/shard_map/while/body/eval_jaxpr/stack | solution.py:213
  173.6 16.9 %reshape.268 = f32[16,65536]{1,0:T(8,128)} reshape(f32[4,512,2,8,32]{4,3,2,1,0:T(8,128)} %copy.182) | data formatting | bytes 8388608 | tf_op jit(solution)/shard_map/while/body/eval_jaxpr/reshape | solution.py:213
  190.4 2.2 broadcast_in_dim.24
  192.7 37.6 %scatter_fusion = f32[12,65536]{1,0:T(8,128)} fusion(f32[12,65536]{1,0:T(8,128)} %broadcast_in_dim.24, s32[16]{0:T(128)S(1)} %fusion.92, f32[16,65536]{1,0:T(8,128)} %reshape.268), kind=kCustom, calls=%fused_computation.1 | custom fusion | flops 1048576 | bytes 12582976 | tf_op jit(solution)/shard_map/while/body/eval_jaxpr/scatter-add | solution.py:216
  230.3 2.8 reshape.246
  234.4 1.9 collective-permute-start.2
  236.3 3.4 collective-permute-start.3
  239.8 11.5 %fusion.31 = bf16[4,128,8,32]{1,3,2,0:T(8,128)(2,1)} fusion(bf16[4,8,128,512]{3,2,1,0:T(8,128)(2,1)} %copy-done, f32[4,8,128,512]{3,2,1,0:T(8,128)} %fusion.41, bf16[4,512,1,8,32]{1,0,4,3,2:T(4,128)(2,1)} %copy-done.10), kind=kOutput, calls=%fused_computation.59 | convolution fusion | flops 149033472 | bytes 13893632 | tf_op jit(solution)/shard_map/while/body/eval_jaxpr/ghqk,gkhe->gqhe/dot_general | solution.py:66
  252.5 2.1 fusion.66
  259.9 112.4 %all-reduce.7.cloned.1.call-done = (f32[256,768]{1,0:T(8,128)}, f32[256,768]{1,0:T(8,128)}, f32[256,256]{1,0:T(8,128)}, f32[256,256]{1,0:T(8,128)}) async-done(((f32[256,768]{1,0:T(8,128)}, f32[256,768]{1,0:T(8,128)}, f32[256,256]{1,0:T(8,128)}, f32[256,256]{1,0:T(8,128)}), (f32[256,768]{1,0:T(8,128)}, f32[256,768]{1,0:T(8,128)}, f32[256,256]{1,0:T(8,128)}, ...) | async-done | bytes 2097168 | tf_op jit(solution)/shard_map/psum | solution.py:239
  373.2 1.8 fusion.29
  375.0 3.8 all-to-all-start.1
  379.8 6.6 %all-to-all-done.1 = bf16[16,32,256]{2,1,0:T(8,128)(2,1)S(1)} async-done(((bf16[16,32,256]{2,1,0:T(8,128)(2,1)}), bf16[16,32,256]{2,1,0:T(8,128)(2,1)S(1)}, u32[]{:S(2)}, u32[]{:S(2)}) %all-to-all-start.1) | async-done | bytes 262176 | tf_op jit(solution)/shard_map/all_to_all | solution.py:190
  387.4 1.7 fusion.102
  390.5 217.7 %all-reduce.5.cloned.1.call-done = (f32[1,256,768]{2,1,0:T(8,128)}, f32[1,256,768]{2,1,0:T(8,128)}, f32[1,256,256]{2,1,0:T(8,128)}, f32[1,256,256]{2,1,0:T(8,128)}) async-done(((f32[1,256,768]{2,1,0:T(8,128)}, f32[1,256,768]{2,1,0:T(8,128)}, f32[1,256,256]{2,1,0:T(8,128)}, f32[1,256,256]{2,1,0:T(8,128)}), (f32[1,256,768]{2,1,0:T(8,128)}, f32[1,256,768]{2,1,0:T(8,128)}, f32[1,256,256]{2,1,0:T(8,128)}, ...) | async-done | bytes 2097168 | tf_op jit(solution)/shard_map/psum | solution.py:238
  608.2 2.7 maximum_multiply_fusion
  (157 shorter events, 42.7 us)
Async XLA Ops:
  7.2 13.2 %copy-start.34 = (bf16[2,256,256]{2,1,0:T(8,128)(2,1)S(1)}, bf16[2,256,256]{2,1,0:T(8,128)(2,1)}, u32[]{:S(2)}) copy-start(bf16[2,256,256]{2,1,0:T(8,128)(2,1)} %param.8) | copy-start | bytes 786436
  7.2 20.1 %copy-start.37 = (s32[2,2,4]{2,1,0:T(2,128)S(1)}, s32[2,2,4]{2,1,0:T(2,128)}, u32[]{:S(2)}) copy-start(s32[2,2,4]{2,1,0:T(2,128)} %param.9) | copy-start | bytes 196
  10.7 0.7 copy-start.19
  13.3 25.3 %collective-permute-start.1 = (bf16[2,256,512]{1,0,2:T(2,128)(2,1)S(1)}, bf16[2,256,512]{1,0,2:T(2,128)(2,1)S(1)}, u32[]{:S(2)}, u32[]{:S(2)}) collective-permute-start(bf16[2,256,512]{1,0,2:T(2,128)(2,1)S(1)} %copy.194), channel_id=1, source_target_pairs={{1,0},{2,1},{3,2},{4,3},{5,4},{6,5},{7,6},{8,7},{9,8},{10,9},{11,1... | collective-permute-start | bytes 1572872 | tf_op jit(solution)/shard_map/ppermute | solution.py:23
  18.4 20.2 %collective-permute-start = (bf16[2,256,512]{1,0,2:T(2,128)(2,1)S(1)}, bf16[2,256,512]{1,0,2:T(2,128)(2,1)}, u32[]{:S(2)}, u32[]{:S(2)}) collective-permute-start(bf16[2,256,512]{1,0,2:T(2,128)(2,1)S(1)} %copy.194), channel_id=1, source_target_pairs={{0,1},{1,2},{2,3},{3,4},{4,5},{5,6},{6,7},{7,8},{8,9},{9,10},{10,1... | collective-permute-start | bytes 1572872 | tf_op jit(solution)/shard_map/ppermute | solution.py:21
  21.3 17.3 %all-to-all-start.2 = ((bf16[2,256,256]{2,0,1:T(2,128)(2,1)}), bf16[2,256,256]{2,0,1:T(2,128)(2,1)S(1)}, u32[]{:S(2)}, u32[]{:S(2)}) async-start(bf16[2,256,256]{2,0,1:T(2,128)(2,1)} %copy.163), calls=%async_computation.2 | async-start | bytes 524288 | tf_op jit(solution)/shard_map/all_to_all | solution.py:184
  28.0 27.9 %copy-start.30 = (bf16[4,128,8,32]{1,0,3,2:T(4,128)(2,1)}, bf16[4,128,8,32]{1,0,3,2:T(4,128)(2,1)S(1)}, u32[]{:S(2)}) copy-start(bf16[4,128,8,32]{1,0,3,2:T(4,128)(2,1)S(1)} %squeeze.57) | copy-start | bytes 786436
  38.6 35.8 %copy-start.15 = (bf16[2,8,32,256]{3,2,0,1:T(8,128)(2,1)}, bf16[2,8,32,256]{3,2,0,1:T(8,128)(2,1)S(1)}, u32[]{:S(2)}) copy-start(bf16[2,8,32,256]{3,2,0,1:T(8,128)(2,1)S(1)} %copy.164) | copy-start | bytes 786436
  55.8 1.0 copy-start.10
  55.9 9.8 %copy-start.1 = (bf16[4,512,1,8,32]{1,0,4,3,2:T(4,128)(2,1)}, bf16[4,512,1,8,32]{1,0,4,3,2:T(4,128)(2,1)S(1)}, u32[]{:S(2)}) copy-start(bf16[4,512,1,8,32]{1,0,4,3,2:T(4,128)(2,1)S(1)} %get-tuple-element.57) | copy-start | bytes 3145732
  65.6 2.0 copy-start
  67.6 1.9 copy-start.11
  67.6 1.9 copy-start.33
  69.3 15.6 %copy-start.27 = (bf16[4,128,8,32]{1,0,3,2:T(4,128)(2,1)}, bf16[4,128,8,32]{1,0,3,2:T(4,128)(2,1)S(1)}, u32[]{:S(2)}) copy-start(bf16[4,128,8,32]{1,0,3,2:T(4,128)(2,1)S(1)} %copy.151) | copy-start | bytes 786436
  69.5 16.2 %copy-start.22 = (bf16[2,256,768]{2,1,0:T(8,128)(2,1)S(1)}, bf16[2,256,768]{2,1,0:T(8,128)(2,1)}, u32[]{:S(2)}) copy-start(bf16[2,256,768]{2,1,0:T(8,128)(2,1)} %param.10) | copy-start | bytes 2359300
  70.8 12.6 %all-to-all-start = ((bf16[2,256,256]{2,0,1:T(2,128)(2,1)}), bf16[2,256,256]{2,0,1:T(2,128)(2,1)S(1)}, u32[]{:S(2)}, u32[]{:S(2)}) async-start(bf16[2,256,256]{2,0,1:T(2,128)(2,1)} %copy.153), calls=%async_computation | async-start | bytes 524288 | tf_op jit(solution)/shard_map/all_to_all | solution.py:183
  85.0 0.7 copy-start.28
  97.0 3.4 copy-start.5
  97.0 3.4 copy-start.21
  100.4 3.2 copy-start.12
  102.8 1.6 copy-start.14
  103.7 1.6 copy-start.13
  114.8 7.6 %copy-start.8 = (f32[8,2,32,256]{3,2,1,0:T(8,128)}, f32[8,2,32,256]{3,2,1,0:T(8,128)S(1)}, u32[]{:S(2)}) copy-start(f32[8,2,32,256]{3,2,1,0:T(8,128)S(1)} %copy.155) | copy-start | bytes 1572868
  114.9 4.3 copy-start.29
  117.7 4.7 copy-start.3
  117.7 4.2 copy-start.23
  117.7 4.7 copy-start.16
  119.2 2.7 copy-start.24
  123.5 11.8 %all-to-all-start.3 = ((bf16[16,32,256]{2,1,0:T(8,128)(2,1)}), bf16[16,32,256]{2,1,0:T(8,128)(2,1)S(1)}, u32[]{:S(2)}, u32[]{:S(2)}) async-start(bf16[16,32,256]{2,1,0:T(8,128)(2,1)} %fusion.58), calls=%async_computation.3 | async-start | bytes 524288 | tf_op jit(solution)/shard_map/all_to_all | solution.py:191
  126.9 245.5 %all-reduce.7.cloned.1.call-start = ((), (), s32[]{:S(2)}) async-start(), calls=%async_computation.5 | async-start | bytes 4194304 | tf_op jit(solution)/shard_map/psum | solution.py:239
  135.3 0.7 copy-start.17
  137.4 3.0 copy-start.2
  140.4 4.5 copy-start.31
  234.4 21.4 %collective-permute-start.2 = (bf16[2,256,512]{2,1,0:T(8,128)(2,1)}, bf16[2,256,512]{2,1,0:T(8,128)(2,1)}, u32[]{:S(2)}, u32[]{:S(2)}) collective-permute-start(bf16[2,256,512]{2,1,0:T(8,128)(2,1)} %get-tuple-element.59), channel_id=1, source_target_pairs={{0,1},{1,2},{2,3},{3,4},{4,5},{5,6},{6,7},{7,8},{8,9},{9,10},{10,1... | collective-permute-start | bytes 1572872 | tf_op jit(solution)/shard_map/ppermute | solution.py:21
  236.3 19.5 %collective-permute-start.3 = (bf16[2,256,512]{2,1,0:T(8,128)(2,1)}, bf16[2,256,512]{2,1,0:T(8,128)(2,1)}, u32[]{:S(2)}, u32[]{:S(2)}) collective-permute-start(bf16[2,256,512]{2,1,0:T(8,128)(2,1)} %get-tuple-element.60), channel_id=1, source_target_pairs={{1,0},{2,1},{3,2},{4,3},{5,4},{6,5},{7,6},{8,7},{9,8},{10,9},{11,1... | collective-permute-start | bytes 1572872 | tf_op jit(solution)/shard_map/ppermute | solution.py:23
  251.3 6.9 %copy-start.20 = (bf16[2,256,256]{2,1,0:T(8,128)(2,1)S(1)}, bf16[2,256,256]{2,1,0:T(8,128)(2,1)}, u32[]{:S(2)}) copy-start(bf16[2,256,256]{2,1,0:T(8,128)(2,1)} %copy-done.19) | copy-start | bytes 786436
  252.5 3.3 copy-start.25
  257.2 1.0 copy-start.6
  258.9 113.5 %copy-start.4 = (bf16[16,32,8,32]{3,2,1,0:T(8,128)(2,1)S(1)}, bf16[16,32,8,32]{3,2,1,0:T(8,128)(2,1)}, u32[]{:S(2)}) copy-start(bf16[16,32,8,32]{3,2,1,0:T(8,128)(2,1)} %copy-done.3) | copy-start | bytes 786436
  259.9 113.3 %copy-start.9 = (f32[8,2,32,256]{3,2,1,0:T(8,128)S(1)}, f32[8,2,32,256]{3,2,1,0:T(8,128)}, u32[]{:S(2)}) copy-start(f32[8,2,32,256]{3,2,1,0:T(8,128)} %copy-done.8) | copy-start | bytes 1572868
  259.9 348.3 %all-reduce.5.cloned.1.call-start = ((), (), s32[]{:S(2)}) async-start(), calls=%async_computation.4 | async-start | bytes 4194304 | tf_op jit(solution)/shard_map/psum | solution.py:238
  372.4 14.7 %copy-start.26 = (bf16[4,128,8,32]{1,0,3,2:T(4,128)(2,1)S(1)}, bf16[4,128,8,32]{1,0,3,2:T(4,128)(2,1)}, u32[]{:S(2)}) copy-start(bf16[4,128,8,32]{1,0,3,2:T(4,128)(2,1)} %copy-done.25) | copy-start | bytes 786436
  372.4 15.0 %copy-start.7 = (f32[2,256,512]{2,1,0:T(8,128)S(1)}, f32[2,256,512]{2,1,0:T(8,128)}, u32[]{:S(2)}) copy-start(f32[2,256,512]{2,1,0:T(8,128)} %copy-done.6) | copy-start | bytes 3145732
  375.0 14.4 %copy-start.18 = (bf16[8,2,32,256]{3,2,0,1:T(8,128)(2,1)S(1)}, bf16[8,2,32,256]{3,2,0,1:T(8,128)(2,1)}, u32[]{:S(2)}) copy-start(bf16[8,2,32,256]{3,2,0,1:T(8,128)(2,1)} %copy-done.17) | copy-start | bytes 786436
  375.0 11.4 %all-to-all-start.1 = ((bf16[16,32,256]{2,1,0:T(8,128)(2,1)}), bf16[16,32,256]{2,1,0:T(8,128)(2,1)S(1)}, u32[]{:S(2)}, u32[]{:S(2)}) async-start(bf16[16,32,256]{2,1,0:T(8,128)(2,1)} %fusion.29), calls=%async_computation.1 | async-start | bytes 524288 | tf_op jit(solution)/shard_map/all_to_all | solution.py:190
  379.8 7.6 %copy-start.32 = (bf16[256,768]{1,0:T(8,128)(2,1)}, bf16[256,768]{1,0:T(8,128)(2,1)S(1)}, u32[]{:S(2)}) copy-start(bf16[256,768]{1,0:T(8,128)(2,1)S(1)} %slice_bitcast_fusion) | copy-start | bytes 1179652
  608.2 2.7 copy-start.35
  608.2 2.7 copy-start.36
Sparse Core Ops, SparseCore 0:
  260.0 112.3 all-reduce.6
  375.2 232.9 all-reduce.4
